TPU v7x, 32 devices: a whole 2x2x4 slice. The times are simulated.
32 devices in a mesh: rep: 2 (over x), fsdp: 2 (over core), seq: 8 (over z, y).
Axes of the slice: x: 2, y: 2, z: 4, core: 2. Of those that a mesh axis runs over, the one named last changes fastest.
Arguments:
- tokens: bfloat16 [2, 4, 2048, 768], P(None, ('rep', 'fsdp'), 'seq'), may hold values from -6 to 6
- lengths: int32 [2, 4, 8], P(None, ('rep', 'fsdp')), may hold values from 1 to 1024, 2048 in all within a row
- ln1_gain: bfloat16 [768], P('fsdp'), may hold values from 0.099609375 to 1.8984375
- ln1_bias: bfloat16 [768], P('fsdp'), may hold values from -3 to 3
- qkv_weight: bfloat16 [768, 2304], P('fsdp'), may hold values from -0.21875 to 0.21875
- q_gain: bfloat16 [64], P('fsdp'), may hold values from 0.099609375 to 1.8984375
- k_gain: bfloat16 [64], P('fsdp'), may hold values from 0.099609375 to 1.8984375
- out_weight: bfloat16 [768, 768], P('fsdp'), may hold values from -1.75 to 1.75
- ln2_gain: bfloat16 [768], P('fsdp'), may hold values from 0.099609375 to 1.8984375
- ln2_bias: bfloat16 [768], P('fsdp'), may hold values from -3 to 3
- up_weight: bfloat16 [768, 3072], P('fsdp'), may hold values from -0.21875 to 0.21875
- down_weight: bfloat16 [3072, 768], P('fsdp'), may hold values from -0.109375 to 0.109375
- cotangent: bfloat16 [2, 4, 2048, 768], P(None, ('rep', 'fsdp'), 'seq'), may hold values from -6 to 6
Outputs:
- output: bfloat16 [2, 4, 2048, 768], P(None, ('rep', 'fsdp'), 'seq')
- grad_tokens: float32 [2, 4, 2048, 768], P(None, ('rep', 'fsdp'), 'seq')
- grad_ln1_gain: float32 [768], P('fsdp')
- grad_ln1_bias: float32 [768], P('fsdp')
- grad_qkv_weight: float32 [768, 2304], P('fsdp')
- grad_q_gain: float32 [64], P('fsdp')
- grad_k_gain: float32 [64], P('fsdp')
- grad_out_weight: float32 [768, 768], P('fsdp')
- grad_ln2_gain: float32 [768], P('fsdp')
- grad_ln2_bias: float32 [768], P('fsdp')
- grad_up_weight: float32 [768, 3072], P('fsdp')
- grad_down_weight: float32 [3072, 768], P('fsdp')
Inputs may be any that keep to these rules, and one draw needn't show every extreme that they name: In each row the first 7 entries are the lengths of its pictures in order and the last one is the padding at the row's end; each row's entries sum to 2048, and each row's largest entry is 1024.
All inputs are finite; a program needn't handle non-finite values.
Results may differ from a plain program's by a relative error of at most 0.014.
Values may be sent and summed in bfloat16 or wider, within the bound.
No kernel may reach another device: no remote copies, remote signals or barrier semaphores. Data moves between devices by JAX's collectives and lax.ppermute only.
A program may use at most 320 MiB of HBM per device.

v0:
```python
from functools import partial
import jax
import jax.numpy as jnp
from jax import lax
from jax.sharding import PartitionSpec as P

H = 12
EPS = 1e-06
MASKED = -1000000000.0


def layer_norm(values, gain, shift):
    center = jnp.mean(values, axis=-1, keepdims=True)
    centred = values - center
    spread = jnp.mean(centred * centred, axis=-1, keepdims=True)
    return centred * lax.rsqrt(spread + EPS) * gain + shift


def head_norm(values, gain):
    return layer_norm(values, gain, 0.0)


def gelu_exact(values):
    return jax.nn.gelu(values, approximate=False)


def picture_ids(lengths, length):
    bounds = jnp.cumsum(lengths, axis=-1)
    places = jnp.arange(length, dtype=jnp.int32)
    ident = jnp.sum((places[:, None] >= bounds[..., None, :-1]).astype(jnp.int32), axis=-1)
    return jnp.where(ident == lengths.shape[-1] - 1, -1, ident)


def split_groups(tensor):
    rows, length, width = tensor.shape
    shaped = tensor.reshape(rows, length, H // 2, 2, width // H)
    return jnp.moveaxis(shaped, 2, 0)


def join_groups(tensor):
    moved = jnp.moveaxis(tensor, 0, 2)
    return moved.reshape(moved.shape[0], moved.shape[1], -1)


def group_scores(q_group, k_group, same, scale):
    scores = (
        jnp.einsum("rqhd,rkhd->rhqk", q_group, k_group, preferred_element_type=jnp.float32) * scale
    )
    return jnp.where(same[:, None], scores, MASKED)


def attend_group(inputs, same, scale):
    q_group, k_group, v_group = inputs
    scores = group_scores(q_group, k_group, same, scale)
    top = jnp.max(scores, axis=-1, keepdims=True)
    expo = jnp.exp(scores - top)
    total = jnp.sum(expo, axis=-1, keepdims=True)
    probs = (expo / total).astype(jnp.bfloat16)
    context = jnp.einsum("rhqk,rkhd->rqhd", probs, v_group, preferred_element_type=jnp.float32)
    return (context, top[..., 0] + jnp.log(total[..., 0]))


def attend_back(inputs, same, scale):
    q_group, k_group, v_group, grad_group, logsum = inputs
    scores = group_scores(q_group, k_group, same, scale)
    probs = jnp.exp(scores - logsum[..., None])
    grad_probs = jnp.einsum(
        "rqhd,rkhd->rhqk", grad_group, v_group, preferred_element_type=jnp.float32
    )
    inner = jnp.sum(probs * grad_probs, axis=-1, keepdims=True)
    grad_scores = (probs * (grad_probs - inner)).astype(jnp.bfloat16)
    grad_q = (
        jnp.einsum("rhqk,rkhd->rqhd", grad_scores, k_group, preferred_element_type=jnp.float32)
        * scale
    )
    grad_k = (
        jnp.einsum("rhqk,rqhd->rkhd", grad_scores, q_group, preferred_element_type=jnp.float32)
        * scale
    )
    grad_v = jnp.einsum(
        "rhqk,rqhd->rkhd",
        probs.astype(jnp.bfloat16),
        grad_group,
        preferred_element_type=jnp.float32,
    )
    return (grad_q, grad_k, grad_v)


def unpack(weights):
    return tuple((member.astype(jnp.float32) if member.ndim == 1 else member for member in weights))


def on_device(
    tokens,
    lengths,
    ln1_gain,
    ln1_bias,
    qkv_weight,
    q_gain,
    k_gain,
    out_weight,
    ln2_gain,
    ln2_bias,
    up_weight,
    down_weight,
    cotangent,
):
    shards = (
        ln1_gain,
        ln1_bias,
        qkv_weight,
        q_gain,
        k_gain,
        out_weight,
        ln2_gain,
        ln2_bias,
        up_weight,
        down_weight,
    )
    micro, rows, local, width = tokens.shape
    head_dim = width // H
    scale = head_dim ** (-0.5)
    length = local * lax.axis_size("seq")
    offset = lax.axis_index("seq") * local

    def fetch():
        return unpack(
            (
                lax.all_gather(shards[0], "fsdp", axis=0, tiled=True),
                lax.all_gather(shards[1], "fsdp", axis=0, tiled=True),
                lax.all_gather(shards[2], "fsdp", axis=0, tiled=True),
                lax.all_gather(shards[3], "fsdp", axis=0, tiled=True),
                lax.all_gather(shards[4], "fsdp", axis=0, tiled=True),
                lax.all_gather(shards[5], "fsdp", axis=0, tiled=True),
                lax.all_gather(shards[6], "fsdp", axis=0, tiled=True),
                lax.all_gather(shards[7], "fsdp", axis=0, tiled=True),
                lax.all_gather(shards[8], "fsdp", axis=0, tiled=True),
                lax.all_gather(shards[9], "fsdp", axis=0, tiled=True),
            )
        )

    outputs = []
    grad_inputs = []
    running = None
    for index in range(micro):
        gathered = fetch()
        g_one, b_one, w_qkv, g_query, g_key, w_out, g_two, b_two, w_up, w_down = gathered
        x_block = tokens[index].astype(jnp.float32)
        ident = picture_ids(lengths[index], length)
        ident_local = lax.dynamic_slice_in_dim(ident, offset, local, 1)
        same = (ident_local[:, :, None] == ident[:, None, :]) & (ident[:, None, :] >= 0)
        valid = (ident_local >= 0).astype(jnp.float32)[..., None]
        norm_one, pull_one = jax.vjp(layer_norm, x_block, g_one, b_one)
        first = norm_one.astype(jnp.bfloat16)
        qkv = jnp.dot(first, w_qkv, preferred_element_type=jnp.float32)
        q_raw = qkv[..., :width].reshape(rows, local, H, head_dim)
        k_raw = qkv[..., width : 2 * width].reshape(rows, local, H, head_dim)
        q_normed, pull_query = jax.vjp(head_norm, q_raw, g_query)
        k_normed, pull_key = jax.vjp(head_norm, k_raw, g_key)
        queries = q_normed.astype(jnp.bfloat16).reshape(rows, local, width)
        keys = k_normed.astype(jnp.bfloat16).reshape(rows, local, width)
        values = qkv[..., 2 * width :].astype(jnp.bfloat16)
        keys_all, values_all = (
            lax.all_gather(keys, "seq", axis=1, tiled=True),
            lax.all_gather(values, "seq", axis=1, tiled=True),
        )
        q_groups = split_groups(queries)
        k_groups = split_groups(keys_all)
        v_groups = split_groups(values_all)
        context, logsum = lax.map(
            partial(attend_group, same=same, scale=scale), (q_groups, k_groups, v_groups)
        )
        attn = (join_groups(context) * valid).astype(jnp.bfloat16)
        middle = x_block + jnp.dot(attn, w_out, preferred_element_type=jnp.float32)
        norm_two, pull_two = jax.vjp(layer_norm, middle, g_two, b_two)
        second = norm_two.astype(jnp.bfloat16)
        upper = jnp.dot(second, w_up, preferred_element_type=jnp.float32)
        active_full, pull_active = jax.vjp(gelu_exact, upper)
        active = active_full.astype(jnp.bfloat16)
        result = middle + jnp.dot(active, w_down, preferred_element_type=jnp.float32)
        outputs.append(result.astype(jnp.bfloat16))
        again = fetch()
        w_qkv, w_out, w_up, w_down = (again[2], again[5], again[8], again[9])
        grad_y = cotangent[index]
        grad_down = jnp.einsum("rsf,rsd->fd", active, grad_y, preferred_element_type=jnp.float32)
        grad_active = jnp.einsum("rsd,fd->rsf", grad_y, w_down, preferred_element_type=jnp.float32)
        (grad_upper,) = pull_active(grad_active)
        grad_upper = grad_upper.astype(jnp.bfloat16)
        grad_up = jnp.einsum("rsd,rsf->df", second, grad_upper, preferred_element_type=jnp.float32)
        grad_second = jnp.einsum(
            "rsf,df->rsd", grad_upper, w_up, preferred_element_type=jnp.float32
        )
        grad_mid_norm, grad_g_two, grad_b_two = pull_two(grad_second)
        grad_middle = grad_y.astype(jnp.float32) + grad_mid_norm
        grad_branch = grad_middle.astype(jnp.bfloat16)
        grad_out = jnp.einsum("rsd,rse->de", attn, grad_branch, preferred_element_type=jnp.float32)
        grad_attn = (
            jnp.einsum("rse,de->rsd", grad_branch, w_out, preferred_element_type=jnp.float32)
            * valid
        ).astype(jnp.bfloat16)
        grad_qg, grad_kg, grad_vg = lax.map(
            partial(attend_back, same=same, scale=scale),
            (q_groups, k_groups, v_groups, split_groups(grad_attn), logsum),
        )
        grad_keys, grad_values = (
            lax.psum_scatter(
                join_groups(grad_kg).astype(jnp.bfloat16), "seq", scatter_dimension=1, tiled=True
            ).astype(jnp.float32),
            lax.psum_scatter(
                join_groups(grad_vg).astype(jnp.bfloat16), "seq", scatter_dimension=1, tiled=True
            ).astype(jnp.float32),
        )
        grad_q_raw, grad_g_query = pull_query(
            join_groups(grad_qg).reshape(rows, local, H, head_dim)
        )
        grad_k_raw, grad_g_key = pull_key(grad_keys.reshape(rows, local, H, head_dim))
        grad_qkv = jnp.concatenate(
            [
                grad_q_raw.reshape(rows, local, width),
                grad_k_raw.reshape(rows, local, width),
                grad_values,
            ],
            axis=-1,
        ).astype(jnp.bfloat16)
        grad_qkv_w = jnp.einsum("rsd,rse->de", first, grad_qkv, preferred_element_type=jnp.float32)
        grad_first = jnp.einsum("rse,de->rsd", grad_qkv, w_qkv, preferred_element_type=jnp.float32)
        grad_x_norm, grad_g_one, grad_b_one = pull_one(grad_first)
        grad_inputs.append(grad_middle + grad_x_norm)
        grads = (
            grad_g_one,
            grad_b_one,
            grad_qkv_w,
            grad_g_query,
            grad_g_key,
            grad_out,
            grad_g_two,
            grad_b_two,
            grad_up,
            grad_down,
        )
        running = grads if index == 0 else jax.tree.map(jnp.add, running, grads)
    owned = lax.psum_scatter(running, "fsdp", scatter_dimension=0, tiled=True)
    running = lax.psum(owned, ("rep", "seq"))
    output = jnp.stack(outputs, axis=0)
    grad_tokens = jnp.stack(grad_inputs, axis=0)
    return (
        output,
        grad_tokens,
        running[0],
        running[1],
        running[2],
        running[3],
        running[4],
        running[5],
        running[6],
        running[7],
        running[8],
        running[9],
    )


def solution(mesh):
    in_specs = (
        P(None, ("rep", "fsdp"), "seq", None),
        P(None, ("rep", "fsdp"), None),
        P("fsdp"),
        P("fsdp"),
        P("fsdp", None),
        P("fsdp"),
        P("fsdp"),
        P("fsdp", None),
        P("fsdp"),
        P("fsdp"),
        P("fsdp", None),
        P("fsdp", None),
        P(None, ("rep", "fsdp"), "seq", None),
    )
    out_specs = (
        P(None, ("rep", "fsdp"), "seq", None),
        P(None, ("rep", "fsdp"), "seq", None),
        P("fsdp"),
        P("fsdp"),
        P("fsdp", None),
        P("fsdp"),
        P("fsdp"),
        P("fsdp", None),
        P("fsdp"),
        P("fsdp"),
        P("fsdp", None),
        P("fsdp", None),
    )
    return jax.shard_map(
        on_device, mesh=mesh, in_specs=in_specs, out_specs=out_specs, check_vma=False
    )
```

profile of v0, /device:TPU:0, one launch (start us, length us, event | category | flops | bytes accessed | tf_op | source)
XLA Modules:
  0.0 1268.5 jit_solution(4192007691853410526)
XLA Ops:
  15.5 9.5 all-gather.13.cloned.1.call-done
  25.0 3.2 convolution_bitcast_fusion.2
  33.9 3.2 convolution_bitcast_fusion.3
  47.8 3.9 multiply_convert_fusion.8
  67.0 23.4 %all-gather.25.cloned.1.call-done = bf16[1,2048,768]{2,1,0:T(8,128)(2,1)} async-done(((bf16[1,256,768]{2,1,0:T(8,128)(2,1)}), bf16[1,2048,768]{2,1,0:T(8,128)(2,1)}) %all-gather.25.cloned.1.call-update) | async-done | bytes 3145744 | tf_op jit(solution)/shard_map/all_gather | solution.py:165
  90.4 4.8 copy.197
  95.3 56.6 %all-gather.27.cloned.1.call-done = bf16[1,2048,768]{2,1,0:T(8,128)(2,1)} async-done(((bf16[1,256,768]{2,1,0:T(8,128)(2,1)}), bf16[1,2048,768]{2,1,0:T(8,128)(2,1)}) %all-gather.27.cloned.1.call-update) | async-done | bytes 3145744 | tf_op jit(solution)/shard_map/all_gather | solution.py:164
  151.9 3.2 copy.205
  156.6 47.0 %while.57 = (s32[]{:T(128)}, f32[6,1,256,2,64]{2,4,3,1,0:T(8,128)}, f32[6,1,2,256]{3,2,1,0:T(2,128)}, bf16[6,1,2048,2,64]{2,4,3,1,0:T(8,128)(2,1)}, bf16[6,1,256...) while((s32[]{:T(128)}, f32[6,1,256,2,64]{2,4,3,1,0:T(8,128)}, ...), condition=%wide.region_25.26_spmd.clone, body=%wide.region_22.25_spmd.clone.sunk | while | flops 282066432 | bytes 15955057 | solution.py:170
  160.9 3.0 fusion.293
  168.8 2.9 fusion.293
  176.6 3.0 fusion.293
  184.4 3.0 fusion.293
  192.3 2.9 fusion.293
  200.1 3.0 fusion.293
  203.6 2.8 copy.210
  211.0 13.5 %all-gather.15.cloned.1.call-done = bf16[1,2048,768]{2,1,0:T(8,128)(2,1)} async-done(((bf16[1,256,768]{2,1,0:T(8,128)(2,1)}), bf16[1,2048,768]{2,1,0:T(8,128)(2,1)}) %all-gather.15.cloned.1.call-update) | async-done | bytes 3145744 | tf_op jit(solution)/shard_map/all_gather | solution.py:165
  224.5 4.7 copy.183
  229.2 56.7 %all-gather.17.cloned.1.call-done = bf16[1,2048,768]{2,1,0:T(8,128)(2,1)} async-done(((bf16[1,256,768]{2,1,0:T(8,128)(2,1)}), bf16[1,2048,768]{2,1,0:T(8,128)(2,1)}) %all-gather.17.cloned.1.call-update) | async-done | bytes 3145744 | tf_op jit(solution)/shard_map/all_gather | solution.py:164
  285.8 3.2 copy.191
  290.6 42.0 %while.56 = (s32[]{:T(128)}, f32[6,1,256,2,64]{2,4,3,1,0:T(8,128)}, f32[6,1,2,256]{3,2,1,0:T(2,128)}, bf16[6,1,2048,2,64]{2,4,3,1,0:T(8,128)(2,1)}, bf16[6,1,256...) while((s32[]{:T(128)}, f32[6,1,256,2,64]{2,4,3,1,0:T(8,128)}, ...), condition=%wide.region_11.12_spmd.clone, body=%wide.region_8.11_spmd.clone.sunk | while | flops 282066432 | bytes 15955057 | solution.py:170
  294.0 3.0 fusion.289
  301.1 2.9 fusion.289
  308.0 3.0 fusion.289
  315.1 3.0 fusion.289
  322.1 2.9 fusion.289
  329.0 2.9 fusion.289
  339.4 12.3 multiply_convert_fusion.2
  351.7 11.5 multiply_convert_fusion.3
  363.3 6.4 add_convert_fusion
  388.8 77.8 %while.59 = (s32[]{:T(128)}, f32[6,1,256,2,64]{2,4,3,1,0:T(8,128)}, bf16[6,1,2048,2,64]{2,4,3,1,0:T(8,128)(2,1)}, bf16[6,1,2048,2,64]{2,4,3,1,0:T(8,128)(2,1)}, ...) while((s32[]{:T(128)}, f32[6,1,256,2,64]{2,4,3,1,0:T(8,128)}, ...), condition=%wide.region_45.46_spmd.clone, body=%wide.region_43.45_spmd.clone.sunk | while | flops 681868800 | bytes 36608192 | solution.py:201
  391.9 2.9 multiply_reduce_fusion.21
  404.8 2.9 multiply_reduce_fusion.21
  417.8 2.9 multiply_reduce_fusion.21
  430.7 2.9 multiply_reduce_fusion.21
  443.6 2.9 multiply_reduce_fusion.21
  456.6 2.9 multiply_reduce_fusion.21
  466.6 4.7 copy.242
  472.0 2.6 fusion.108
  481.6 59.9 %while.58 = (s32[]{:T(128)}, f32[6,1,256,2,64]{2,4,3,1,0:T(8,128)}, bf16[6,1,2048,2,64]{2,4,3,1,0:T(8,128)(2,1)}, bf16[6,1,2048,2,64]{2,4,3,1,0:T(8,128)(2,1)}, ...) while((s32[]{:T(128)}, f32[6,1,256,2,64]{2,4,3,1,0:T(8,128)}, ...), condition=%wide.region_32.33_spmd.clone, body=%wide.region_30.32_spmd.clone.sunk | while | flops 681868800 | bytes 36595848 | solution.py:201
  541.5 4.7 copy.223
  548.1 2.8 copy.229
  552.8 2.8 copy.248
  559.6 3.1 fusion.206
  562.8 5.3 convolution_add_fusion.2
  569.2 3.0 fusion.172
  572.3 5.2 convolution_add_fusion.1
  600.6 20.7 %reduce-scatter.9.cloned.1.call-done = bf16[1,256,768]{2,1,0:T(8,128)(2,1)} async-done(((bf16[1,2048,768]{2,1,0:T(8,128)(2,1)}), bf16[1,256,768]{2,1,0:T(8,128)(2,1)}) %reduce-scatter.9.cloned.1.call-update) | async-done | bytes 393232 | tf_op jit(solution)/shard_map/reduce_scatter | solution.py:206
  631.7 5.1 multiply_reduce_fusion.5
  636.7 62.2 %reduce-scatter.11.cloned.1.call-done = bf16[1,256,768]{2,1,0:T(8,128)(2,1)} async-done(((bf16[1,2048,768]{2,1,0:T(8,128)(2,1)}), bf16[1,256,768]{2,1,0:T(8,128)(2,1)}) %reduce-scatter.11.cloned.1.call-update) | async-done | bytes 393232 | tf_op jit(solution)/shard_map/reduce_scatter | solution.py:209
  699.0 5.5 fusion.159
  707.1 69.6 %reduce-scatter.15.cloned.1.call-done = bf16[1,256,768]{2,1,0:T(8,128)(2,1)} async-done(((bf16[1,2048,768]{2,1,0:T(8,128)(2,1)}), bf16[1,256,768]{2,1,0:T(8,128)(2,1)}) %reduce-scatter.15.cloned.1.call-update) | async-done | bytes 393232 | tf_op jit(solution)/shard_map/reduce_scatter | solution.py:209
  776.7 7.4 convolution_add_fusion
  784.5 4.3 reduce-scatter.19.cloned.1.call-done
  788.8 20.7 %reduce-scatter.21.cloned.1.call-done = f32[384,3072]{1,0:T(8,128)} async-done(((f32[768,3072]{1,0:T(8,128)}), f32[384,3072]{1,0:T(8,128)}) %reduce-scatter.21.cloned.1.call-update) | async-done | bytes 4718608 | tf_op jit(solution)/shard_map/reduce_scatter | solution.py:242
  809.5 20.7 %reduce-scatter.23.cloned.1.call-done = f32[1536,768]{1,0:T(8,128)} async-done(((f32[3072,768]{1,0:T(8,128)}), f32[1536,768]{1,0:T(8,128)}) %reduce-scatter.23.cloned.1.call-update) | async-done | bytes 4718608 | tf_op jit(solution)/shard_map/reduce_scatter | solution.py:242
  830.2 19.3 %reduce-scatter.17.cloned.1.call-done = f32[384,2304]{1,0:T(8,128)} async-done(((f32[768,2304]{1,0:T(8,128)}), f32[384,2304]{1,0:T(8,128)}) %reduce-scatter.17.cloned.1.call-update) | async-done | bytes 3538960 | tf_op jit(solution)/shard_map/reduce_scatter | solution.py:242
  852.6 4.3 fusion.110
  857.0 3.8 fusion.111
  863.1 3.4 fusion.158
  870.3 4.2 all-reduce.10
  874.9 47.1 %all-reduce.8 = (f32[384]{0:T(512)}, f32[384]{0:T(512)}, f32[32]{0:T(128)}, f32[32]{0:T(128)}, f32[384]{0:T(512)}, /*index=5*/f32[384]{0:T(512)}) all-reduce(f32[384]{0:T(512)S(1)} %dynamic-slice.3, f32[384]{0:T(512)S(1)} %dynamic-slice.5, f32[32]{0:T(128)S(1)} %dynamic-slice.7, ...), channel_id=1, replica_groups=mesh['rep'=2,'fsdp'=2,'seq'=8] {'rep','seq'}, use_global_device_ids=true, to_apply=%region_57.58 | all-reduce | flops 1600 | bytes 12800 | tf_op jit(solution)/shard_map/psum | solution.py:243
  925.4 325.2 %all-reduce.14.cloned.1.call-done = (f32[384,2304]{1,0:T(8,128)}, f32[384,768]{1,0:T(8,128)}, f32[384,3072]{1,0:T(8,128)}, f32[1536,768]{1,0:T(8,128)}) async-done(((f32[384,2304]{1,0:T(8,128)}, f32[384,768]{1,0:T(8,128)}, f32[384,3072]{1,0:T(8,128)}, f32[1536,768]{1,0:T(8,128)}), (f32[384,2304]{1,0:T(8,128)}, f32[384,768]{1,0:T(8,128)}, f32[384,3072]{1,0:T(8,128)}, ...) | async-done | bytes 14155792 | tf_op jit(solution)/shard_map/psum | solution.py:243
  1250.7 4.2 copy.314
  (748 shorter events, 315.9 us)
Async XLA Ops:
  7.2 17.8 %all-gather.13.cloned.1.call-start = ((), (), s32[]{:S(2)}) async-start(), calls=%async_computation.8 | async-start | bytes 5308416 | tf_op jit(solution)/shard_map/all_gather | solution.py:131
  7.9 82.5 %all-gather.25.cloned.1.call-start = ((), (), s32[]{:S(2)}) async-start(), calls=%async_computation.14 | async-start | bytes 3538944 | tf_op jit(solution)/shard_map/all_gather | solution.py:165
  10.7 23.3 %copy-start.65 = (f32[768]{0:T(1024)}, f32[768]{0:T(1024)S(1)}, u32[]{:S(2)}) copy-start(f32[768]{0:T(1024)S(1)} %reshape.2349) | copy-start | bytes 9220
  13.2 20.7 %copy-start.63 = (f32[768]{0:T(1024)}, f32[768]{0:T(1024)S(1)}, u32[]{:S(2)}) copy-start(f32[768]{0:T(1024)S(1)} %reshape.2348) | copy-start | bytes 9220
  14.5 13.7 %copy-start.116 = (f32[256]{0:T(256)}, f32[256]{0:T(256)S(1)}, u32[]{:S(2)}) copy-start(f32[256]{0:T(256)S(1)} %get-tuple-element.627) | copy-start | bytes 3076
  14.5 19.4 %copy-start.112 = (f32[256]{0:T(256)}, f32[256]{0:T(256)S(1)}, u32[]{:S(2)}) copy-start(f32[256]{0:T(256)S(1)} %get-tuple-element.628) | copy-start | bytes 3076
  14.9 19.0 %copy-start.139 = (f32[256]{0:T(256)}, f32[256]{0:T(256)S(1)}, u32[]{:S(2)}) copy-start(f32[256]{0:T(256)S(1)} %get-tuple-element.456) | copy-start | bytes 3076
  15.5 12.7 copy-start.119
  15.5 13.6 %copy-start.155 = (u32[32]{0:T(128)S(1)}, u32[32]{0:T(128)}, u32[]{:S(2)}) copy-start(u32[32]{0:T(128)} %constant.217) | copy-start | bytes 388
  15.5 14.9 %copy-start.169 = (bf16[32]{0:T(256)(128)(2,1)S(1)}, bf16[32]{0:T(256)(128)(2,1)}, u32[]{:S(2)}) copy-start(bf16[32]{0:T(256)(128)(2,1)} %param.26) | copy-start | bytes 196
  15.5 15.1 %copy-start.170 = (bf16[32]{0:T(256)(128)(2,1)S(1)}, bf16[32]{0:T(256)(128)(2,1)}, u32[]{:S(2)}) copy-start(bf16[32]{0:T(256)(128)(2,1)} %param.27) | copy-start | bytes 196
  28.2 8.9 copy-start.23
  29.1 122.8 %all-gather.27.cloned.1.call-start = ((), (), s32[]{:S(2)}) async-start(), calls=%async_computation.15 | async-start | bytes 3538944 | tf_op jit(solution)/shard_map/all_gather | solution.py:164
  33.4 25.1 %copy-start.161 = (bf16[64]{0:T(256)(128)(2,1)}, bf16[64]{0:T(256)(128)(2,1)S(1)}, u32[]{:S(2)}) copy-start(bf16[64]{0:T(256)(128)(2,1)S(1)} %get-tuple-element.564) | copy-start | bytes 388
  33.9 13.9 %copy-start.110 = (f32[768]{0:T(1024)}, f32[768]{0:T(1024)S(1)}, u32[]{:S(2)}) copy-start(f32[768]{0:T(1024)S(1)} %mul.1115) | copy-start | bytes 9220
  43.7 8.1 copy-start.69
  51.8 154.7 %all-gather.19.cloned.1.call-start = ((), (), s32[]{:S(2)}) async-start(), calls=%async_computation.11 | async-start | bytes 1769472 | tf_op jit(solution)/shard_map/all_gather | solution.py:134
  52.4 8.6 copy-start.158
  52.4 11.6 copy-start.48
  52.4 172.1 %all-gather.15.cloned.1.call-start = ((), (), s32[]{:S(2)}) async-start(), calls=%async_computation.9 | async-start | bytes 3538944 | tf_op jit(solution)/shard_map/all_gather | solution.py:165
  54.5 231.4 %all-gather.17.cloned.1.call-start = ((), (), s32[]{:S(2)}) async-start(), calls=%async_computation.10 | async-start | bytes 3538944 | tf_op jit(solution)/shard_map/all_gather | solution.py:164
  55.0 284.3 %all-gather.21.cloned.1.call-start = ((), (), s32[]{:S(2)}) async-start(), calls=%async_computation.12 | async-start | bytes 7077888 | tf_op jit(solution)/shard_map/all_gather | solution.py:137
  55.8 9.4 copy-start.47
  55.8 307.4 %all-gather.23.cloned.1.call-start = ((), (), s32[]{:S(2)}) async-start(), calls=%async_computation.13 | async-start | bytes 7077888 | tf_op jit(solution)/shard_map/all_gather | solution.py:138
  56.6 542.8 %reduce-scatter.13.cloned.1.call-start = ((), (), s32[]{:S(2)}) async-start(), calls=%async_computation.18 | async-start | bytes 3538944 | tf_op jit(solution)/shard_map/reduce_scatter | solution.py:206
  65.2 30.0 %copy-start.100 = (f32[256,6,2]{0,2,1:T(2,128)}, f32[256,6,2]{0,2,1:T(2,128)S(1)}, u32[]{:S(2)}) copy-start(f32[256,6,2]{0,2,1:T(2,128)S(1)} %rsqrt.97) | copy-start | bytes 36868
  65.5 29.8 %copy-start.5 = (f32[1,256,768]{1,2,0:T(8,128)}, f32[1,256,768]{1,2,0:T(8,128)S(1)}, u32[]{:S(2)}) copy-start(f32[1,256,768]{1,2,0:T(8,128)S(1)} %copy.198) | copy-start | bytes 2359300
  65.6 29.7 %copy-start.73 = (f32[256,12]{0,1:T(8,128)}, f32[256,12]{0,1:T(8,128)S(1)}, u32[]{:S(2)}) copy-start(f32[256,12]{0,1:T(8,128)S(1)} %broadcast_multiply_fusion.1) | copy-start | bytes 36868
  65.6 29.6 %copy-start.102 = (f32[256,6,2]{0,2,1:T(2,128)}, f32[256,6,2]{0,2,1:T(2,128)S(1)}, u32[]{:S(2)}) copy-start(f32[256,6,2]{0,2,1:T(2,128)S(1)} %div.200) | copy-start | bytes 36868
  65.7 29.5 %copy-start.94 = (f32[256,12]{0,1:T(8,128)}, f32[256,12]{0,1:T(8,128)S(1)}, u32[]{:S(2)}) copy-start(f32[256,12]{0,1:T(8,128)S(1)} %multiply_reduce_fusion.14) | copy-start | bytes 36868
  65.8 29.5 %copy-start.108 = (f32[256,6,2]{0,2,1:T(2,128)}, f32[256,6,2]{0,2,1:T(2,128)S(1)}, u32[]{:S(2)}) copy-start(f32[256,6,2]{0,2,1:T(2,128)S(1)} %add.307) | copy-start | bytes 36868
  65.8 29.5 %copy-start.104 = (f32[256,6,2]{0,2,1:T(2,128)}, f32[256,6,2]{0,2,1:T(2,128)S(1)}, u32[]{:S(2)}) copy-start(f32[256,6,2]{0,2,1:T(2,128)S(1)} %rsqrt.101) | copy-start | bytes 36868
  203.6 25.6 %copy-start = (bf16[6,1,2048,2,64]{2,4,3,1,0:T(8,128)(2,1)}, bf16[6,1,2048,2,64]{2,4,3,1,0:T(8,128)(2,1)S(1)}, u32[]{:S(2)}) copy-start(bf16[6,1,2048,2,64]{2,4,3,1,0:T(8,128)(2,1)S(1)} %get-tuple-element.1084) | copy-start | bytes 9437188
  339.3 12.4 copy-start.19
  339.3 12.4 copy-start.75
  339.3 12.4 copy-start.80
  339.3 12.4 copy-start.122
  339.3 12.4 copy-start.130
  339.3 12.4 copy-start.166
  363.2 8.0 copy-start.171
  363.3 8.0 copy-start.172
  471.3 149.9 %reduce-scatter.9.cloned.1.call-start = ((), (), s32[]{:S(2)}) async-start(), calls=%async_computation.16 | async-start | bytes 3538944 | tf_op jit(solution)/shard_map/reduce_scatter | solution.py:206
  546.2 152.7 %reduce-scatter.11.cloned.1.call-start = ((), (), s32[]{:S(2)}) async-start(), calls=%async_computation.17 | async-start | bytes 3538944 | tf_op jit(solution)/shard_map/reduce_scatter | solution.py:209
  550.9 225.8 %reduce-scatter.15.cloned.1.call-start = ((), (), s32[]{:S(2)}) async-start(), calls=%async_computation.19 | async-start | bytes 3538944 | tf_op jit(solution)/shard_map/reduce_scatter | solution.py:209
  555.6 233.2 %reduce-scatter.19.cloned.1.call-start = ((), (), s32[]{:S(2)}) async-start(), calls=%async_computation.21 | async-start | bytes 3538944 | tf_op jit(solution)/shard_map/reduce_scatter | solution.py:242
  559.5 250.0 %reduce-scatter.21.cloned.1.call-start = ((), (), s32[]{:S(2)}) async-start(), calls=%async_computation.22 | async-start | bytes 14155776 | tf_op jit(solution)/shard_map/reduce_scatter | solution.py:242
  568.1 262.1 %reduce-scatter.23.cloned.1.call-start = ((), (), s32[]{:S(2)}) async-start(), calls=%async_computation.23 | async-start | bytes 14155776 | tf_op jit(solution)/shard_map/reduce_scatter | solution.py:242
  577.5 272.0 %reduce-scatter.17.cloned.1.call-start = ((), (), s32[]{:S(2)}) async-start(), calls=%async_computation.20 | async-start | bytes 10616832 | tf_op jit(solution)/shard_map/reduce_scatter | solution.py:242
  596.9 26.4 %copy-start.8 = (f32[1,256,768]{1,2,0:T(8,128)S(1)}, f32[1,256,768]{1,2,0:T(8,128)}, u32[]{:S(2)}) copy-start(f32[1,256,768]{1,2,0:T(8,128)} %copy-done.7) | copy-start | bytes 2359300
  596.9 26.4 %copy-start.68 = (f32[256,12]{0,1:T(8,128)S(1)}, f32[256,12]{0,1:T(8,128)}, u32[]{:S(2)}) copy-start(f32[256,12]{0,1:T(8,128)} %copy-done.67) | copy-start | bytes 36868
  598.2 26.4 %copy-start.89 = (f32[256,12]{0,1:T(8,128)S(1)}, f32[256,12]{0,1:T(8,128)}, u32[]{:S(2)}) copy-start(f32[256,12]{0,1:T(8,128)} %copy-done.88) | copy-start | bytes 36868
  598.2 26.5 %copy-start.10 = (f32[1,256,768]{1,2,0:T(8,128)S(1)}, f32[1,256,768]{1,2,0:T(8,128)}, u32[]{:S(2)}) copy-start(f32[1,256,768]{1,2,0:T(8,128)} %copy-done.9) | copy-start | bytes 2359300
  598.2 26.5 %copy-start.70 = (f32[256,12]{0,1:T(8,128)S(1)}, f32[256,12]{0,1:T(8,128)}, u32[]{:S(2)}) copy-start(f32[256,12]{0,1:T(8,128)} %copy-done.69) | copy-start | bytes 36868
  598.2 26.5 %copy-start.85 = (f32[256,12]{0,1:T(8,128)S(1)}, f32[256,12]{0,1:T(8,128)}, u32[]{:S(2)}) copy-start(f32[256,12]{0,1:T(8,128)} %copy-done.84) | copy-start | bytes 36868
  600.6 25.8 %copy-start.91 = (f32[256,12]{0,1:T(8,128)S(1)}, f32[256,12]{0,1:T(8,128)}, u32[]{:S(2)}) copy-start(f32[256,12]{0,1:T(8,128)} %copy-done.90) | copy-start | bytes 36868
  600.6 25.8 %copy-start.87 = (f32[256,12]{0,1:T(8,128)S(1)}, f32[256,12]{0,1:T(8,128)}, u32[]{:S(2)}) copy-start(f32[256,12]{0,1:T(8,128)} %copy-done.86) | copy-start | bytes 36868
  631.6 67.3 %copy-start.2 = (bf16[2,1,256,768]{3,2,1,0:T(8,128)(2,1)S(1)}, bf16[2,1,256,768]{3,2,1,0:T(8,128)(2,1)}, u32[]{:S(2)}) copy-start(bf16[2,1,256,768]{3,2,1,0:T(8,128)(2,1)} %param.21) | copy-start | bytes 2359300
  631.6 67.3 %copy-start.64 = (f32[768]{0:T(1024)S(1)}, f32[768]{0:T(1024)}, u32[]{:S(2)}) copy-start(f32[768]{0:T(1024)} %copy-done.63) | copy-start | bytes 9220
  631.7 67.3 %copy-start.66 = (f32[768]{0:T(1024)S(1)}, f32[768]{0:T(1024)}, u32[]{:S(2)}) copy-start(f32[768]{0:T(1024)} %copy-done.65) | copy-start | bytes 9220
  631.7 67.3 %copy-start.113 = (f32[256]{0:T(256)S(1)}, f32[256]{0:T(256)}, u32[]{:S(2)}) copy-start(f32[256]{0:T(256)} %copy-done.112) | copy-start | bytes 3076
  784.1 466.5 %all-reduce.14.cloned.1.call-start = ((), (), s32[]{:S(2)}) async-start(), calls=%async_computation.24 | async-start | bytes 28311552 | tf_op jit(solution)/shard_map/psum | solution.py:243
  866.6 55.5 %copy-start.28 = (bf16[2,1,256,768]{3,2,1,0:T(8,128)(2,1)S(1)}, bf16[2,1,256,768]{3,2,1,0:T(8,128)(2,1)}, u32[]{:S(2)}) copy-start(bf16[2,1,256,768]{3,2,1,0:T(8,128)(2,1)} %param.33) | copy-start | bytes 2359300
  866.6 55.4 %copy-start.30 = (f32[256,768]{1,0:T(8,128)S(1)}, f32[256,768]{1,0:T(8,128)}, u32[]{:S(2)}) copy-start(f32[256,768]{1,0:T(8,128)} %copy-done.29) | copy-start | bytes 2359300
  866.6 55.4 %copy-start.32 = (f32[256,768]{1,0:T(8,128)S(1)}, f32[256,768]{1,0:T(8,128)}, u32[]{:S(2)}) copy-start(f32[256,768]{1,0:T(8,128)} %copy-done.31) | copy-start | bytes 2359300
  (141 other events, 426.8 us)
Sparse Core Ops, SparseCore 0:
  9.5 15.4 all-gather.12
  29.2 61.1 all-gather.24
  93.2 58.6 all-gather.26
  153.3 7.8 all-gather.18
  163.2 61.2 all-gather.14
  227.1 58.6 all-gather.16
  287.4 13.0 all-gather.20
  302.0 15.6 all-gather.22
  471.4 73.0 reduce-scatter.12
  547.9 73.2 reduce-scatter.8
  625.4 73.4 reduce-scatter.10
  702.9 73.7 reduce-scatter.14
  779.6 9.2 reduce-scatter.18
  791.0 18.5 reduce-scatter.20
  811.6 18.5 reduce-scatter.22
  832.4 17.0 reduce-scatter.16
  855.8 394.8 all-reduce.13
where the time goes:
time: 1280 us; the launch traced here: 1270 us
  waiting for transfers between devices  706 us (55%)
  matrix products  268 us (21%)
  local copies, waits for them, and re-layouts  131 us (10%)
  other arithmetic  81.9 us (6%)
  blocking collectives  61.2 us (5%)
  between operations  18.8 us (1%)
    psum x1, waiting for transfers between devices, on_device(): running = lax.psum(owned, ('rep', 'seq'))  325 us
    reduce_scatter x2, waiting for transfers between devices, on_device(): lax.psum_scatter(join_groups(grad_vg).astype(jnp.bfloat16), 'seq', scatte...  132 us
    all_gather x2, waiting for transfers between devices, on_device(): lax.all_gather(keys, 'seq', axis=1, tiled=True)  113 us
    reduce_scatter x4, waiting for transfers between devices, on_device(): owned = lax.psum_scatter(running, 'fsdp', scatter_dimension=0, tiled=True)  65 us
    psum x1, blocking collectives, on_device(): running = lax.psum(owned, ('rep', 'seq'))  47.1 us
    dot_general x24, matrix products, group_scores(): jnp.einsum('rqhd,rkhd->rhqk', q_group, k_group, preferred_element_type=jn...  46.2 us
    all_gather x2, waiting for transfers between devices, on_device(): lax.all_gather(values, 'seq', axis=1, tiled=True)  36.9 us
    dot_general x12, matrix products, attend_group(): jnp.einsum('rhqk,rkhd->rqhd', probs, v_group, preferred_element_type=jnp....  35.5 us
  transfers between devices with their start and end apart: 17, of which 13 were waited for; matrix products, arithmetic and copies ran while one was open for 27% of the time, Pallas kernels for 0%

commit v1 on v0

--- a/solution.py
+++ b/solution.py
@@ -7,6 +7,27 @@
 H = 12
 EPS = 1e-06
 MASKED = -1000000000.0
+
+
+def in_order(blocks, dim):
+    blocks = jnp.moveaxis(blocks, 0, dim)
+    shape = blocks.shape
+    return blocks.reshape(*shape[:dim], shape[dim] * shape[dim + 1], *shape[dim + 2 :])
+
+
+def doubled(shard, axis):
+    size, here = (lax.axis_size(axis), lax.axis_index(axis))
+    blocks, bit = (shard[None], 1)
+    while bit < size:
+        other = lax.ppermute(blocks, axis, [(i, i ^ bit) for i in range(size)])
+        low = here & bit == 0
+        blocks = jnp.concatenate([jnp.where(low, blocks, other), jnp.where(low, other, blocks)])
+        bit *= 2
+    return blocks
+
+
+def collect(x, axis, dim):
+    return in_order(doubled(x, axis), dim)
 
 
 def layer_norm(values, gain, shift):
@@ -162,7 +183,7 @@
         values = qkv[..., 2 * width :].astype(jnp.bfloat16)
         keys_all, values_all = (
             lax.all_gather(keys, "seq", axis=1, tiled=True),
-            lax.all_gather(values, "seq", axis=1, tiled=True),
+            collect(values, "seq", 1),
         )
         q_groups = split_groups(queries)
         k_groups = split_groups(keys_all)

time: 1280 us -> 1360 us (1.062)
  waiting for transfers between devices: 706 us -> 746 us
  local copies, waits for them, and re-layouts: 131 us -> 151 us
    ppermute x0 -> x6, waiting for transfers between devices: none -> 197 us  [doubled(): other = lax.ppermute(blocks, axis, [(i, i ^ bit) for i in range(size)])]
    all_gather x2, waiting for transfers between devices: 113 us -> 0.01 us  [on_device(): lax.all_gather(keys, 'seq', axis=1, tiled=True)]
    all_gather x2 -> x0, waiting for transfers between devices: 36.9 us -> none  [on_device(): lax.all_gather(values, 'seq', axis=1, tiled=True)]
    unnamed x369 -> x363, local copies, waits for them, and re-layouts: 31.3 us -> 35.8 us
  transfers between devices with their start and end apart: 17 -> 21, of which waited for: 13 -> 15; matrix products, arithmetic and copies ran while one was open for 27% -> 27% of each run, Pallas kernels for 0% -> 0%
where the time goes in v1:
time: 1360 us; the launch traced here: 1350 us
  waiting for transfers between devices  746 us (55%)
  matrix products  268 us (20%)
  local copies, waits for them, and re-layouts  151 us (11%)
  other arithmetic  94.7 us (7%)
  blocking collectives  61.7 us (5%)
  between operations  18.7 us (1%)
    psum x1, waiting for transfers between devices, on_device(): running = lax.psum(owned, ('rep', 'seq'))  325 us
    ppermute x6, waiting for transfers between devices, doubled(): other = lax.ppermute(blocks, axis, [(i, i ^ bit) for i in range(size)])  197 us
    reduce_scatter x2, waiting for transfers between devices, on_device(): lax.psum_scatter(join_groups(grad_vg).astype(jnp.bfloat16), 'seq', scatte...  131 us
    reduce_scatter x4, waiting for transfers between devices, on_device(): owned = lax.psum_scatter(running, 'fsdp', scatter_dimension=0, tiled=True)  65.1 us
    psum x1, blocking collectives, on_device(): running = lax.psum(owned, ('rep', 'seq'))  47.1 us
    dot_general x24, matrix products, group_scores(): jnp.einsum('rqhd,rkhd->rhqk', q_group, k_group, preferred_element_type=jn...  46.2 us
    unnamed x363, local copies, waits for them, and re-layouts  35.8 us
    dot_general x12, matrix products, attend_group(): jnp.einsum('rhqk,rkhd->rqhd', probs, v_group, preferred_element_type=jnp....  35.3 us
  transfers between devices with their start and end apart: 21, of which 15 were waited for; matrix products, arithmetic and copies ran while one was open for 27% of the time, Pallas kernels for 0%

profile of v1, /device:TPU:0, one launch (start us, length us, event | category | flops | bytes accessed | tf_op | source)
XLA Modules:
  0.0 1348.3 jit_solution(1112840923881391249)
XLA Ops:
  16.9 3.0 all-reduce.11
  25.0 3.2 convolution_bitcast_fusion.3
  33.9 3.2 convolution_bitcast_fusion.2
  46.1 3.8 multiply_convert_fusion.8
  62.2 7.6 collective-permute-done.3
  82.2 27.7 %collective-permute-done.4 = bf16[2,1,256,768]{3,2,1,0:T(8,128)(2,1)} collective-permute-done((bf16[2,1,256,768]{3,2,1,0:T(8,128)(2,1)S(1)}, bf16[2,1,256,768]{3,2,1,0:T(8,128)(2,1)}, u32[]{:S(2)}, u32[]{:S(2)}) %collective-permute-start.4) | collective-permute-done | bytes 786464 | tf_op jit(solution)/shard_map/ppermute | solution.py:22
  113.8 39.4 %collective-permute-done.1 = bf16[2,1,256,768]{3,2,1,0:T(8,128)(2,1)} collective-permute-done((bf16[2,1,256,768]{3,2,1,0:T(8,128)(2,1)}, bf16[2,1,256,768]{3,2,1,0:T(8,128)(2,1)}, u32[]{:S(2)}, u32[]{:S(2)}) %collective-permute-start.1) | collective-permute-done | bytes 786464 | tf_op jit(solution)/shard_map/ppermute | solution.py:22
  162.3 99.8 %collective-permute-done.5 = bf16[4,1,256,768]{3,2,1,0:T(8,128)(2,1)} collective-permute-done((bf16[4,1,256,768]{3,2,1,0:T(8,128)(2,1)}, bf16[4,1,256,768]{3,2,1,0:T(8,128)(2,1)}, u32[]{:S(2)}, u32[]{:S(2)}) %collective-permute-start.5) | collective-permute-done | bytes 1572896 | tf_op jit(solution)/shard_map/ppermute | solution.py:22
  264.0 3.5 copy.197
  267.5 6.0 reshape_reshape_transpose.7
  273.5 21.3 %collective-permute-done.2 = bf16[4,1,256,768]{3,2,1,0:T(8,128)(2,1)} collective-permute-done((bf16[4,1,256,768]{3,2,1,0:T(8,128)(2,1)}, bf16[4,1,256,768]{3,2,1,0:T(8,128)(2,1)}, u32[]{:S(2)}, u32[]{:S(2)}) %collective-permute-start.2) | collective-permute-done | bytes 1572896 | tf_op jit(solution)/shard_map/ppermute | solution.py:22
  296.9 3.4 copy.183
  300.2 5.9 reshape_reshape_transpose.6
  306.1 3.2 copy.205
  310.9 46.9 %while.57 = (s32[]{:T(128)}, f32[6,1,256,2,64]{2,4,3,1,0:T(8,128)}, f32[6,1,2,256]{3,2,1,0:T(2,128)}, bf16[6,1,2048,2,64]{2,4,3,1,0:T(8,128)(2,1)}, bf16[6,1,256...) while((s32[]{:T(128)}, f32[6,1,256,2,64]{2,4,3,1,0:T(8,128)}, ...), condition=%wide.region_25.26_spmd.clone, body=%wide.region_22.25_spmd.clone.sunk | while | flops 282066432 | bytes 15955057 | solution.py:191
  315.2 3.0 fusion.295
  323.0 3.0 fusion.295
  330.8 3.0 fusion.295
  338.6 3.0 fusion.295
  346.4 3.0 fusion.295
  354.3 3.0 fusion.295
  365.1 3.2 copy.191
  369.9 41.9 %while.56 = (s32[]{:T(128)}, f32[6,1,256,2,64]{2,4,3,1,0:T(8,128)}, f32[6,1,2,256]{3,2,1,0:T(2,128)}, bf16[6,1,2048,2,64]{2,4,3,1,0:T(8,128)(2,1)}, bf16[6,1,256...) while((s32[]{:T(128)}, f32[6,1,256,2,64]{2,4,3,1,0:T(8,128)}, ...), condition=%wide.region_11.12_spmd.clone, body=%wide.region_8.11_spmd.clone.sunk | while | flops 282066432 | bytes 15955057 | solution.py:191
  373.3 2.9 fusion.291
  380.3 2.9 fusion.291
  387.2 2.9 fusion.291
  394.2 2.9 fusion.291
  401.1 2.9 fusion.291
  408.1 2.9 fusion.291
  418.6 11.7 multiply_convert_fusion.2
  430.4 11.4 multiply_convert_fusion.3
  441.8 6.4 add_convert_fusion
  467.3 77.8 %while.59 = (s32[]{:T(128)}, f32[6,1,256,2,64]{2,4,3,1,0:T(8,128)}, bf16[6,1,2048,2,64]{2,4,3,1,0:T(8,128)(2,1)}, bf16[6,1,2048,2,64]{2,4,3,1,0:T(8,128)(2,1)}, ...) while((s32[]{:T(128)}, f32[6,1,256,2,64]{2,4,3,1,0:T(8,128)}, ...), condition=%wide.region_45.46_spmd.clone, body=%wide.region_43.45_spmd.clone.sunk | while | flops 681868800 | bytes 36608192 | solution.py:222
  470.4 2.9 multiply_reduce_fusion.21
  483.3 2.9 multiply_reduce_fusion.21
  496.3 2.9 multiply_reduce_fusion.21
  509.2 2.9 multiply_reduce_fusion.21
  522.2 2.9 multiply_reduce_fusion.21
  535.1 2.9 multiply_reduce_fusion.21
  545.1 4.6 copy.242
  560.2 59.9 %while.58 = (s32[]{:T(128)}, f32[6,1,256,2,64]{2,4,3,1,0:T(8,128)}, bf16[6,1,2048,2,64]{2,4,3,1,0:T(8,128)(2,1)}, bf16[6,1,2048,2,64]{2,4,3,1,0:T(8,128)(2,1)}, ...) while((s32[]{:T(128)}, f32[6,1,256,2,64]{2,4,3,1,0:T(8,128)}, ...), condition=%wide.region_32.33_spmd.clone, body=%wide.region_30.32_spmd.clone.sunk | while | flops 681868800 | bytes 36595848 | solution.py:222
  620.1 4.7 copy.223
  626.7 2.8 copy.229
  638.3 3.1 fusion.208
  641.5 5.3 convolution_add_fusion.2
  647.9 3.0 fusion.174
  650.9 5.1 convolution_add_fusion.1
  679.2 22.6 %reduce-scatter.9.cloned.1.call-done = bf16[1,256,768]{2,1,0:T(8,128)(2,1)} async-done(((bf16[1,2048,768]{2,1,0:T(8,128)(2,1)}), bf16[1,256,768]{2,1,0:T(8,128)(2,1)}) %reduce-scatter.9.cloned.1.call-update) | async-done | bytes 393232 | tf_op jit(solution)/shard_map/reduce_scatter | solution.py:227
  712.2 5.0 multiply_reduce_fusion.5
  717.2 61.7 %reduce-scatter.11.cloned.1.call-done = bf16[1,256,768]{2,1,0:T(8,128)(2,1)} async-done(((bf16[1,2048,768]{2,1,0:T(8,128)(2,1)}), bf16[1,256,768]{2,1,0:T(8,128)(2,1)}) %reduce-scatter.11.cloned.1.call-update) | async-done | bytes 393232 | tf_op jit(solution)/shard_map/reduce_scatter | solution.py:230
  779.0 5.5 fusion.159
  787.1 69.3 %reduce-scatter.15.cloned.1.call-done = bf16[1,256,768]{2,1,0:T(8,128)(2,1)} async-done(((bf16[1,2048,768]{2,1,0:T(8,128)(2,1)}), bf16[1,256,768]{2,1,0:T(8,128)(2,1)}) %reduce-scatter.15.cloned.1.call-update) | async-done | bytes 393232 | tf_op jit(solution)/shard_map/reduce_scatter | solution.py:230
  856.4 7.4 convolution_add_fusion
  864.1 4.3 reduce-scatter.19.cloned.1.call-done
  868.4 20.7 %reduce-scatter.21.cloned.1.call-done = f32[384,3072]{1,0:T(8,128)} async-done(((f32[768,3072]{1,0:T(8,128)}), f32[384,3072]{1,0:T(8,128)}) %reduce-scatter.21.cloned.1.call-update) | async-done | bytes 4718608 | tf_op jit(solution)/shard_map/reduce_scatter | solution.py:263
  889.1 20.8 %reduce-scatter.23.cloned.1.call-done = f32[1536,768]{1,0:T(8,128)} async-done(((f32[3072,768]{1,0:T(8,128)}), f32[1536,768]{1,0:T(8,128)}) %reduce-scatter.23.cloned.1.call-update) | async-done | bytes 4718608 | tf_op jit(solution)/shard_map/reduce_scatter | solution.py:263
  910.0 19.3 %reduce-scatter.17.cloned.1.call-done = f32[384,2304]{1,0:T(8,128)} async-done(((f32[768,2304]{1,0:T(8,128)}), f32[384,2304]{1,0:T(8,128)}) %reduce-scatter.17.cloned.1.call-update) | async-done | bytes 3538960 | tf_op jit(solution)/shard_map/reduce_scatter | solution.py:263
  932.3 4.3 fusion.110
  936.7 3.8 fusion.111
  942.8 3.4 fusion.158
  950.0 4.2 all-reduce.10
  954.6 47.1 %all-reduce.8 = (f32[384]{0:T(512)}, f32[384]{0:T(512)}, f32[32]{0:T(128)}, f32[32]{0:T(128)}, f32[384]{0:T(512)}, /*index=5*/f32[384]{0:T(512)}) all-reduce(f32[384]{0:T(512)S(1)} %dynamic-slice.3, f32[384]{0:T(512)S(1)} %dynamic-slice.5, f32[32]{0:T(128)S(1)} %dynamic-slice.7, ...), channel_id=1, replica_groups=mesh['rep'=2,'fsdp'=2,'seq'=8] {'rep','seq'}, use_global_device_ids=true, to_apply=%region_57.58 | all-reduce | flops 1600 | bytes 12800 | tf_op jit(solution)/shard_map/psum | solution.py:264
  1005.2 325.2 %all-reduce.14.cloned.1.call-done = (f32[384,2304]{1,0:T(8,128)}, f32[384,768]{1,0:T(8,128)}, f32[384,3072]{1,0:T(8,128)}, f32[1536,768]{1,0:T(8,128)}) async-done(((f32[384,2304]{1,0:T(8,128)}, f32[384,768]{1,0:T(8,128)}, f32[384,3072]{1,0:T(8,128)}, f32[1536,768]{1,0:T(8,128)}), (f32[384,2304]{1,0:T(8,128)}, f32[384,768]{1,0:T(8,128)}, f32[384,3072]{1,0:T(8,128)}, ...) | async-done | bytes 14155792 | tf_op jit(solution)/shard_map/psum | solution.py:264
  1330.4 4.2 copy.314
  (761 shorter events, 355.4 us)
Async XLA Ops:
  7.2 14.3 %copy-start.1 = (bf16[2,1,256,768]{3,2,1,0:T(8,128)(2,1)S(1)}, bf16[2,1,256,768]{3,2,1,0:T(8,128)(2,1)}, u32[]{:S(2)}) copy-start(bf16[2,1,256,768]{3,2,1,0:T(8,128)(2,1)} %param.21) | copy-start | bytes 2359300
  7.2 17.8 %all-gather.11.cloned.1.call-start = ((), (), s32[]{:S(2)}) async-start(), calls=%async_computation.8 | async-start | bytes 5308416 | tf_op jit(solution)/shard_map/all_gather | solution.py:152
  7.9 298.2 %all-gather.21.cloned.1.call-start = ((), (), s32[]{:S(2)}) async-start(), calls=%async_computation.13 | async-start | bytes 3538944 | tf_op jit(solution)/shard_map/all_gather | solution.py:185
  10.7 23.2 %copy-start.69 = (f32[768]{0:T(1024)}, f32[768]{0:T(1024)S(1)}, u32[]{:S(2)}) copy-start(f32[768]{0:T(1024)S(1)} %reshape.2341) | copy-start | bytes 9220
  13.2 20.6 %copy-start.67 = (f32[768]{0:T(1024)}, f32[768]{0:T(1024)S(1)}, u32[]{:S(2)}) copy-start(f32[768]{0:T(1024)S(1)} %reshape.2340) | copy-start | bytes 9220
  19.9 8.3 copy-start.162
  20.0 26.1 %copy-start.111 = (f32[768]{0:T(1024)}, f32[768]{0:T(1024)S(1)}, u32[]{:S(2)}) copy-start(f32[768]{0:T(1024)S(1)} %mul.1115) | copy-start | bytes 9220
  21.4 12.4 copy-start.117
  22.4 11.4 copy-start.120
  38.9 11.0 copy-start.73
  50.0 310.6 %all-gather.15.cloned.1.call-start = ((), (), s32[]{:S(2)}) async-start(), calls=%async_computation.10 | async-start | bytes 1769472 | tf_op jit(solution)/shard_map/all_gather | solution.py:155
  50.7 314.3 %all-gather.13.cloned.1.call-start = ((), (), s32[]{:S(2)}) async-start(), calls=%async_computation.9 | async-start | bytes 3538944 | tf_op jit(solution)/shard_map/all_gather | solution.py:185
  51.3 367.2 %all-gather.17.cloned.1.call-start = ((), (), s32[]{:S(2)}) async-start(), calls=%async_computation.11 | async-start | bytes 7077888 | tf_op jit(solution)/shard_map/all_gather | solution.py:158
  51.9 21.0 %copy-start.160 = (bf16[64]{0:T(256)(128)(2,1)S(1)}, bf16[64]{0:T(256)(128)(2,1)}, u32[]{:S(2)}) copy-start(bf16[64]{0:T(256)(128)(2,1)} %get-tuple-element.564) | copy-start | bytes 388
  51.9 389.9 %all-gather.19.cloned.1.call-start = ((), (), s32[]{:S(2)}) async-start(), calls=%async_computation.12 | async-start | bytes 7077888 | tf_op jit(solution)/shard_map/all_gather | solution.py:159
  52.5 625.5 %reduce-scatter.13.cloned.1.call-start = ((), (), s32[]{:S(2)}) async-start(), calls=%async_computation.16 | async-start | bytes 3538944 | tf_op jit(solution)/shard_map/reduce_scatter | solution.py:227
  53.9 15.9 %collective-permute-start.3 = (bf16[1,1,256,768]{3,2,1,0:T(8,128)(2,1)S(1)}, bf16[1,1,256,768]{3,2,1,0:T(8,128)(2,1)S(1)}, u32[]{:S(2)}, u32[]{:S(2)}) collective-permute-start(bf16[1,1,256,768]{3,2,1,0:T(8,128)(2,1)S(1)} %fusion.164), channel_id=1, source_target_pairs={{0,1},{1,0},{2,3},{3,2},{4,5},{5,4},{6,7},{7,6},{8,9},{9,8},{10,11... | collective-permute-start | bytes 1179656 | tf_op jit(solution)/shard_map/ppermute | solution.py:22
  61.9 16.1 %collective-permute-start = (bf16[1,1,256,768]{3,2,1,0:T(8,128)(2,1)}, bf16[1,1,256,768]{3,2,1,0:T(8,128)(2,1)}, u32[]{:S(2)}, u32[]{:S(2)}) collective-permute-start(bf16[1,1,256,768]{3,2,1,0:T(8,128)(2,1)} %fusion.163), channel_id=1, source_target_pairs={{0,1},{1,0},{2,3},{3,2},{4,5},{5,4},{6,7},{7,6},{8,9},{9,8},{10,11... | collective-permute-start | bytes 1179656 | tf_op jit(solution)/shard_map/ppermute | solution.py:22
  70.7 39.1 %copy-start.47 = (bf16[1,1,256,768]{3,2,1,0:T(8,128)(2,1)S(1)}, bf16[1,1,256,768]{3,2,1,0:T(8,128)(2,1)}, u32[]{:S(2)}) copy-start(bf16[1,1,256,768]{3,2,1,0:T(8,128)(2,1)} %copy-done.46) | copy-start | bytes 1179652
  70.7 39.1 %collective-permute-start.4 = (bf16[2,1,256,768]{3,2,1,0:T(8,128)(2,1)S(1)}, bf16[2,1,256,768]{3,2,1,0:T(8,128)(2,1)}, u32[]{:S(2)}, u32[]{:S(2)}) collective-permute-start(bf16[2,1,256,768]{3,2,1,0:T(8,128)(2,1)S(1)} %pad_maximum_fusion.8), channel_id=1, source_target_pairs={{0,2},{1,3},{2,0},{3,1},{4,6},{5,7},{6,4},{7,5},{8,10},{9,11},{10,... | collective-permute-start | bytes 2359304 | tf_op jit(solution)/shard_map/ppermute | solution.py:22
  76.7 83.6 %copy-start.3 = (f32[1,256,768]{1,2,0:T(8,128)}, f32[1,256,768]{1,2,0:T(8,128)S(1)}, u32[]{:S(2)}) copy-start(f32[1,256,768]{1,2,0:T(8,128)S(1)} %copy.184) | copy-start | bytes 2359300
  80.4 72.8 %collective-permute-start.1 = (bf16[2,1,256,768]{3,2,1,0:T(8,128)(2,1)}, bf16[2,1,256,768]{3,2,1,0:T(8,128)(2,1)}, u32[]{:S(2)}, u32[]{:S(2)}) collective-permute-start(bf16[2,1,256,768]{3,2,1,0:T(8,128)(2,1)} %pad_maximum_fusion.7), channel_id=1, source_target_pairs={{0,2},{1,3},{2,0},{3,1},{4,6},{5,7},{6,4},{7,5},{8,10},{9,11},{10,... | collective-permute-start | bytes 2359304 | tf_op jit(solution)/shard_map/ppermute | solution.py:22
  82.2 30.2 %copy-start.75 = (f32[256,12]{0,1:T(8,128)}, f32[256,12]{0,1:T(8,128)S(1)}, u32[]{:S(2)}) copy-start(f32[256,12]{0,1:T(8,128)S(1)} %broadcast_multiply_fusion.3) | copy-start | bytes 36868
  111.1 42.1 %copy-start.49 = (bf16[1,1,256,768]{3,2,1,0:T(8,128)(2,1)S(1)}, bf16[1,1,256,768]{3,2,1,0:T(8,128)(2,1)}, u32[]{:S(2)}) copy-start(bf16[1,1,256,768]{3,2,1,0:T(8,128)(2,1)} %copy-done.48) | copy-start | bytes 1179652
  112.4 149.7 %collective-permute-start.5 = (bf16[4,1,256,768]{3,2,1,0:T(8,128)(2,1)}, bf16[4,1,256,768]{3,2,1,0:T(8,128)(2,1)}, u32[]{:S(2)}, u32[]{:S(2)}) collective-permute-start(bf16[4,1,256,768]{3,2,1,0:T(8,128)(2,1)} %pad_maximum_fusion.3), channel_id=1, source_target_pairs={{0,4},{1,5},{2,6},{3,7},{4,0},{5,1},{6,2},{7,3},{8,12},{9,13},{10,... | collective-permute-start | bytes 4718600 | tf_op jit(solution)/shard_map/ppermute | solution.py:22
  112.5 44.1 %copy-start.96 = (f32[256,12]{0,1:T(8,128)}, f32[256,12]{0,1:T(8,128)S(1)}, u32[]{:S(2)}) copy-start(f32[256,12]{0,1:T(8,128)S(1)} %multiply_reduce_fusion.17) | copy-start | bytes 36868
  156.6 138.1 %collective-permute-start.2 = (bf16[4,1,256,768]{3,2,1,0:T(8,128)(2,1)}, bf16[4,1,256,768]{3,2,1,0:T(8,128)(2,1)}, u32[]{:S(2)}, u32[]{:S(2)}) collective-permute-start(bf16[4,1,256,768]{3,2,1,0:T(8,128)(2,1)} %pad_maximum_fusion.2), channel_id=1, source_target_pairs={{0,4},{1,5},{2,6},{3,7},{4,0},{5,1},{6,2},{7,3},{8,12},{9,13},{10,... | collective-permute-start | bytes 4718600 | tf_op jit(solution)/shard_map/ppermute | solution.py:22
  158.7 105.0 %copy-start.5 = (f32[1,256,768]{1,2,0:T(8,128)}, f32[1,256,768]{1,2,0:T(8,128)S(1)}, u32[]{:S(2)}) copy-start(f32[1,256,768]{1,2,0:T(8,128)S(1)} %copy.198) | copy-start | bytes 2359300
  267.5 27.2 %copy-start.35 = (bf16[2,1,256,768]{3,2,1,0:T(8,128)(2,1)S(1)}, bf16[2,1,256,768]{3,2,1,0:T(8,128)(2,1)}, u32[]{:S(2)}) copy-start(bf16[2,1,256,768]{3,2,1,0:T(8,128)(2,1)} %copy-done.34) | copy-start | bytes 2359300
  267.5 27.2 %copy-start.37 = (bf16[2,1,256,768]{3,2,1,0:T(8,128)(2,1)S(1)}, bf16[2,1,256,768]{3,2,1,0:T(8,128)(2,1)}, u32[]{:S(2)}) copy-start(bf16[2,1,256,768]{3,2,1,0:T(8,128)(2,1)} %copy-done.36) | copy-start | bytes 2359300
  418.5 11.8 copy-start.19
  418.5 11.8 copy-start.79
  418.6 11.8 copy-start.84
  418.6 11.8 copy-start.123
  418.6 11.8 copy-start.131
  418.6 11.8 copy-start.165
  441.8 8.0 copy-start.168
  441.8 8.0 copy-start.169
  549.8 152.0 %reduce-scatter.9.cloned.1.call-start = ((), (), s32[]{:S(2)}) async-start(), calls=%async_computation.14 | async-start | bytes 3538944 | tf_op jit(solution)/shard_map/reduce_scatter | solution.py:227
  624.8 154.0 %reduce-scatter.11.cloned.1.call-start = ((), (), s32[]{:S(2)}) async-start(), calls=%async_computation.15 | async-start | bytes 3538944 | tf_op jit(solution)/shard_map/reduce_scatter | solution.py:230
  629.5 226.8 %reduce-scatter.15.cloned.1.call-start = ((), (), s32[]{:S(2)}) async-start(), calls=%async_computation.17 | async-start | bytes 3538944 | tf_op jit(solution)/shard_map/reduce_scatter | solution.py:230
  634.3 234.2 %reduce-scatter.19.cloned.1.call-start = ((), (), s32[]{:S(2)}) async-start(), calls=%async_computation.19 | async-start | bytes 3538944 | tf_op jit(solution)/shard_map/reduce_scatter | solution.py:263
  638.2 250.9 %reduce-scatter.21.cloned.1.call-start = ((), (), s32[]{:S(2)}) async-start(), calls=%async_computation.20 | async-start | bytes 14155776 | tf_op jit(solution)/shard_map/reduce_scatter | solution.py:263
  646.8 263.2 %reduce-scatter.23.cloned.1.call-start = ((), (), s32[]{:S(2)}) async-start(), calls=%async_computation.21 | async-start | bytes 14155776 | tf_op jit(solution)/shard_map/reduce_scatter | solution.py:263
  656.1 7.8 copy-start.4
  656.1 7.8 copy-start.6
  656.1 7.8 copy-start.16
  656.1 273.1 %reduce-scatter.17.cloned.1.call-start = ((), (), s32[]{:S(2)}) async-start(), calls=%async_computation.18 | async-start | bytes 10616832 | tf_op jit(solution)/shard_map/reduce_scatter | solution.py:263
  675.5 28.2 %copy-start.8 = (f32[1,256,768]{1,2,0:T(8,128)S(1)}, f32[1,256,768]{1,2,0:T(8,128)}, u32[]{:S(2)}) copy-start(f32[1,256,768]{1,2,0:T(8,128)} %copy-done.7) | copy-start | bytes 2359300
  675.5 28.2 %copy-start.72 = (f32[256,12]{0,1:T(8,128)S(1)}, f32[256,12]{0,1:T(8,128)}, u32[]{:S(2)}) copy-start(f32[256,12]{0,1:T(8,128)} %copy-done.71) | copy-start | bytes 36868
  676.8 28.3 %copy-start.93 = (f32[256,12]{0,1:T(8,128)S(1)}, f32[256,12]{0,1:T(8,128)}, u32[]{:S(2)}) copy-start(f32[256,12]{0,1:T(8,128)} %copy-done.92) | copy-start | bytes 36868
  676.8 28.4 %copy-start.10 = (f32[1,256,768]{1,2,0:T(8,128)S(1)}, f32[1,256,768]{1,2,0:T(8,128)}, u32[]{:S(2)}) copy-start(f32[1,256,768]{1,2,0:T(8,128)} %copy-done.9) | copy-start | bytes 2359300
  676.8 28.4 %copy-start.74 = (f32[256,12]{0,1:T(8,128)S(1)}, f32[256,12]{0,1:T(8,128)}, u32[]{:S(2)}) copy-start(f32[256,12]{0,1:T(8,128)} %copy-done.73) | copy-start | bytes 36868
  676.8 28.4 %copy-start.89 = (f32[256,12]{0,1:T(8,128)S(1)}, f32[256,12]{0,1:T(8,128)}, u32[]{:S(2)}) copy-start(f32[256,12]{0,1:T(8,128)} %copy-done.88) | copy-start | bytes 36868
  679.2 27.7 %copy-start.95 = (f32[256,12]{0,1:T(8,128)S(1)}, f32[256,12]{0,1:T(8,128)}, u32[]{:S(2)}) copy-start(f32[256,12]{0,1:T(8,128)} %copy-done.94) | copy-start | bytes 36868
  679.2 27.7 %copy-start.91 = (f32[256,12]{0,1:T(8,128)S(1)}, f32[256,12]{0,1:T(8,128)}, u32[]{:S(2)}) copy-start(f32[256,12]{0,1:T(8,128)} %copy-done.90) | copy-start | bytes 36868
  712.1 66.7 %copy-start.2 = (bf16[2,1,256,768]{3,2,1,0:T(8,128)(2,1)S(1)}, bf16[2,1,256,768]{3,2,1,0:T(8,128)(2,1)}, u32[]{:S(2)}) copy-start(bf16[2,1,256,768]{3,2,1,0:T(8,128)(2,1)} %param.21) | copy-start | bytes 2359300
  712.1 66.7 %copy-start.68 = (f32[768]{0:T(1024)S(1)}, f32[768]{0:T(1024)}, u32[]{:S(2)}) copy-start(f32[768]{0:T(1024)} %copy-done.67) | copy-start | bytes 9220
  712.1 66.7 %copy-start.70 = (f32[768]{0:T(1024)S(1)}, f32[768]{0:T(1024)}, u32[]{:S(2)}) copy-start(f32[768]{0:T(1024)} %copy-done.69) | copy-start | bytes 9220
  712.2 66.7 %copy-start.114 = (f32[256]{0:T(256)S(1)}, f32[256]{0:T(256)}, u32[]{:S(2)}) copy-start(f32[256]{0:T(256)} %copy-done.113) | copy-start | bytes 3076
  863.8 466.6 %all-reduce.14.cloned.1.call-start = ((), (), s32[]{:S(2)}) async-start(), calls=%async_computation.22 | async-start | bytes 28311552 | tf_op jit(solution)/shard_map/psum | solution.py:264
  946.3 55.5 %copy-start.29 = (bf16[2,1,256,768]{3,2,1,0:T(8,128)(2,1)S(1)}, bf16[2,1,256,768]{3,2,1,0:T(8,128)(2,1)}, u32[]{:S(2)}) copy-start(bf16[2,1,256,768]{3,2,1,0:T(8,128)(2,1)} %param.33) | copy-start | bytes 2359300
  946.3 55.4 %copy-start.31 = (f32[256,768]{1,0:T(8,128)S(1)}, f32[256,768]{1,0:T(8,128)}, u32[]{:S(2)}) copy-start(f32[256,768]{1,0:T(8,128)} %copy-done.30) | copy-start | bytes 2359300
  946.4 55.4 %copy-start.33 = (f32[256,768]{1,0:T(8,128)S(1)}, f32[256,768]{1,0:T(8,128)}, u32[]{:S(2)}) copy-start(f32[256,768]{1,0:T(8,128)} %copy-done.32) | copy-start | bytes 2359300
  (141 other events, 420.3 us)
Sparse Core Ops, SparseCore 0:
  9.5 15.4 all-gather.10
  50.1 95.3 all-gather.20
  147.0 7.0 all-gather.14
  156.2 113.9 all-gather.12
  271.6 13.2 all-gather.16
  286.3 15.6 all-gather.18
  549.9 74.7 reduce-scatter.12
  628.3 73.4 reduce-scatter.8
  705.3 73.4 reduce-scatter.10
  782.9 73.4 reduce-scatter.14
  859.2 9.1 reduce-scatter.18
  870.6 18.5 reduce-scatter.20
  891.4 18.5 reduce-scatter.22
  912.1 17.0 reduce-scatter.16
  935.5 394.8 all-reduce.13
